TPU v7x, 32 devices: a whole 2x2x4 slice. The times are simulated.
32 devices in a mesh: lat: 8 (over z, y), lev: 4 (over x, core).
Axes of the slice: x: 2, y: 2, z: 4, core: 2. Of those that a mesh axis runs over, the one named last changes fastest.
Arguments:
- tracer: float32 [2, 4, 384, 1152], P(None, 'lev', 'lat'), may hold values from 0.1 to 2
- east_courant: float32 [4, 384, 1152], P('lev', 'lat'), may hold values from -0.8 to 0.8
- north_courant: float32 [4, 384, 1152], P('lev', 'lat'), may hold values from -0.8 to 0.8
- fall_speed: float32 [2, 4, 384, 1152], P(None, 'lev', 'lat'), may hold values from 0.05 to 0.6
Outputs:
- tracer_out: float32 [2, 4, 384, 1152], P(None, 'lev', 'lat')
- deposit: float32 [2, 384, 1152], P(None, 'lat', 'lev')
All inputs are finite; a program needn't handle non-finite values.
Results may differ from a plain program's by a relative error of at most 0.0003.
Values sent between devices are 32-bit elements; how exact they have to be, the bound alone decides.
No kernel may reach another device: no remote copies, remote signals or barrier semaphores. Data moves between devices by JAX's collectives and lax.ppermute only.
A program may use at most 64 MiB of HBM per device.

v0:
```python
import jax
import jax.numpy as jnp
from jax import lax
from jax.sharding import PartitionSpec as P

HSUB = 4
SETTLE_SUBSTEPS = 6


def passed_along(block, axis, distance):
    devices = range(lax.axis_size(axis))
    route = [(i - distance, i) for i in devices if i - distance in devices]
    return lax.ppermute(block, axis, route)


def extended(block, sides, width):
    for axis, dim in sides:
        count = lax.axis_size(axis)
        forward = [(i, i + 1) for i in range(count - 1)]
        backward = [(target, source) for source, target in forward]
        low = lax.ppermute(
            lax.slice_in_dim(block, block.shape[dim] - width, None, axis=dim), axis, forward
        )
        high = lax.ppermute(lax.slice_in_dim(block, 0, width, axis=dim), axis, backward)
        block = jnp.concatenate([low, block, high], axis=dim)
    return block


def limiter_face_value(outer_west, inner_west, inner_east, outer_east):
    interp = 7.0 / 12.0 * (inner_west + inner_east) - 1.0 / 12.0 * (outer_west + outer_east)
    return jnp.clip(
        interp, jnp.minimum(inner_west, inner_east), jnp.maximum(inner_west, inner_east)
    )


def window_for_cell(source, start, length, axis_dim):
    return lax.slice_in_dim(source, start, start + length, axis=axis_dim)


def sweep(halo_padded_field, courant, axis_dim):
    cells = halo_padded_field.shape[axis_dim] - 6
    faces = limiter_face_value(
        window_for_cell(halo_padded_field, 0, cells + 3, axis_dim),
        window_for_cell(halo_padded_field, 1, cells + 3, axis_dim),
        window_for_cell(halo_padded_field, 2, cells + 3, axis_dim),
        window_for_cell(halo_padded_field, 3, cells + 3, axis_dim),
    )
    middle = window_for_cell(halo_padded_field, 2, cells + 2, axis_dim)
    west_face = window_for_cell(faces, 0, cells + 2, axis_dim)
    east_face = window_for_cell(faces, 1, cells + 2, axis_dim)
    spread = east_face - west_face
    curvature = 6.0 * middle - 3.0 * (west_face + east_face)
    courant_abs = jnp.abs(courant)
    shape_term = 1.0 - 2.0 / 3.0 * courant_abs
    from_west = window_for_cell(east_face, 0, cells + 1, axis_dim) - 0.5 * courant_abs * (
        window_for_cell(spread, 0, cells + 1, axis_dim)
        - shape_term * window_for_cell(curvature, 0, cells + 1, axis_dim)
    )
    from_east = window_for_cell(west_face, 1, cells + 1, axis_dim) + 0.5 * courant_abs * (
        window_for_cell(spread, 1, cells + 1, axis_dim)
        + shape_term * window_for_cell(curvature, 1, cells + 1, axis_dim)
    )
    face_flux_values = courant * jnp.where(courant >= 0, from_west, from_east)
    return window_for_cell(halo_padded_field, 3, cells, axis_dim) - (
        window_for_cell(face_flux_values, 1, cells, axis_dim)
        - window_for_cell(face_flux_values, 0, cells, axis_dim)
    )


def zonal(field, east_courant):
    last_dim = field.ndim - 1
    width = field.shape[last_dim]
    halo_padded_field = jnp.concatenate(
        [
            window_for_cell(field, width - 3, 3, last_dim),
            field,
            window_for_cell(field, 0, 3, last_dim),
        ],
        last_dim,
    )
    cour_dim = east_courant.ndim - 1
    courant = jnp.concatenate(
        [window_for_cell(east_courant, width - 1, 1, cour_dim), east_courant], cour_dim
    )
    return sweep(halo_padded_field, courant, last_dim)


def settle_flat(column_mass, fall_speed):
    deposit = jnp.zeros_like(column_mass[:, 0])
    for settle_substep in range(SETTLE_SUBSTEPS):
        speeds = fall_speed * (1.0 + 0.5 * jnp.tanh(column_mass))
        face_flux_values = speeds * column_mass
        inflow = jnp.concatenate(
            [jnp.zeros_like(face_flux_values[:, :1]), face_flux_values[:, :-1]], 1
        )
        column_mass = column_mass + inflow - face_flux_values
        deposit = deposit + face_flux_values[:, -1]
    return (column_mass, deposit)


def columns_settle(split_portions):
    column_mass, speed_piece = split_portions
    shape_full = column_mass.shape
    flat_shape = (shape_full[0], shape_full[1], shape_full[2] * shape_full[3])
    settled, deposit = settle_flat(column_mass.reshape(flat_shape), speed_piece.reshape(flat_shape))
    returned = lax.all_to_all(
        settled.reshape(shape_full), "lev", split_axis=1, concat_axis=3, tiled=True
    )
    return (returned, deposit.reshape((shape_full[0], shape_full[2], shape_full[3])))


def on_device(tracer, east_courant, north_courant, fall_speed):
    band_rows = tracer.shape[2]
    all_rows = band_rows * lax.axis_size("lat")
    first_row = lax.axis_index("lat") * band_rows
    row_ids = first_row + jnp.arange(band_rows, dtype=jnp.int32)
    north_faces = jnp.where(
        (row_ids == all_rows - 1)[None, :, None], jnp.zeros_like(north_courant), north_courant
    )
    southern_row = passed_along(north_faces[:, band_rows - 1 :, :], "lat", 1)
    face_cour = jnp.concatenate([southern_row, north_faces], 1)
    field = tracer
    for settle_substep in range(HSUB):
        field = zonal(field, east_courant)
        halo_padded_field = extended(field, (("lat", 2),), 3)
        field = sweep(halo_padded_field, face_cour, 2)
    field, deposit = columns_settle(
        (
            lax.all_to_all(field, "lev", split_axis=3, concat_axis=1, tiled=True),
            lax.all_to_all(fall_speed, "lev", split_axis=3, concat_axis=1, tiled=True),
        )
    )
    field = zonal(field, east_courant)
    halo_padded_field = extended(field, (("lat", 2),), 3)
    field = sweep(halo_padded_field, face_cour, 2)
    return (field, deposit)


def solution(mesh):
    in_specs = (
        P(None, "lev", "lat", None),
        P("lev", "lat", None),
        P("lev", "lat", None),
        P(None, "lev", "lat", None),
    )
    out_specs = (P(None, "lev", "lat", None), P(None, "lat", "lev"))
    return jax.shard_map(
        on_device, mesh=mesh, in_specs=in_specs, out_specs=out_specs, check_vma=False
    )
```

profile of v0, /device:TPU:0, one launch (start us, length us, event | category | flops | bytes accessed | tf_op | source)
XLA Modules:
  0.0 129.7 jit_solution(10379016936662951680)
XLA Ops:
  1.8 4.9 %collective-permute-start = (f32[1,1,1152]{2,1,0:T(1,128)S(1)}, f32[1,1,1152]{2,1,0:T(1,128)S(1)}, u32[]{:S(2)}, u32[]{:S(2)}) collective-permute-start(f32[1,1,1152]{2,1,0:T(1,128)S(1)} %slice.702), channel_id=1, source_target_pairs={{0,4},{4,8},{8,12},{12,16},{16,20},{20,24},{24,28},{1,5},{5,9},{9,... | collective-permute-start | bytes 13832 | tf_op jit(solution)/shard_map/ppermute | solution.py:13
  11.7 3.4 %collective-permute-start.1 = (f32[2,1,3,1152]{3,2,1,0:T(4,128)S(1)}, f32[2,1,3,1152]{3,2,1,0:T(4,128)S(1)}, u32[]{:S(2)}, u32[]{:S(2)}) collective-permute-start(f32[2,1,3,1152]{3,2,1,0:T(4,128)S(1)} %get-tuple-element.46), channel_id=1, source_target_pairs={{0,4},{4,8},{8,12},{12,16},{16,20},{20,24},{24,28},{1,5},{5,9},{9,... | collective-permute-start | bytes 82952 | tf_op jit(solution)/shard_map/ppermute | solution.py:21
  15.1 1.3 collective-permute-start.2
  16.7 4.2 %collective-permute-done.2 = f32[2,1,3,1152]{3,2,1,0:T(4,128)S(1)} collective-permute-done((f32[2,1,3,1152]{3,2,1,0:T(4,128)S(1)}, f32[2,1,3,1152]{3,2,1,0:T(4,128)S(1)}, u32[]{:S(2)}, u32[]{:S(2)}) %collective-permute-start.2) | collective-permute-done | bytes 27680 | tf_op jit(solution)/shard_map/ppermute | solution.py:24
  23.7 4.3 %collective-permute-start.3 = (f32[2,1,3,1152]{3,2,1,0:T(4,128)S(1)}, f32[2,1,3,1152]{3,2,1,0:T(4,128)S(1)}, u32[]{:S(2)}, u32[]{:S(2)}) collective-permute-start(f32[2,1,3,1152]{3,2,1,0:T(4,128)S(1)} %get-tuple-element.42), channel_id=1, source_target_pairs={{0,4},{4,8},{8,12},{12,16},{16,20},{20,24},{24,28},{1,5},{5,9},{9,... | collective-permute-start | bytes 82952 | tf_op jit(solution)/shard_map/ppermute | solution.py:21
  28.0 1.3 collective-permute-start.4
  29.6 4.2 %collective-permute-done.4 = f32[2,1,3,1152]{3,2,1,0:T(4,128)S(1)} collective-permute-done((f32[2,1,3,1152]{3,2,1,0:T(4,128)S(1)}, f32[2,1,3,1152]{3,2,1,0:T(4,128)S(1)}, u32[]{:S(2)}, u32[]{:S(2)}) %collective-permute-start.4) | collective-permute-done | bytes 27680 | tf_op jit(solution)/shard_map/ppermute | solution.py:24
  36.6 3.4 %collective-permute-start.5 = (f32[2,1,3,1152]{3,2,1,0:T(4,128)S(1)}, f32[2,1,3,1152]{3,2,1,0:T(4,128)S(1)}, u32[]{:S(2)}, u32[]{:S(2)}) collective-permute-start(f32[2,1,3,1152]{3,2,1,0:T(4,128)S(1)} %get-tuple-element.38), channel_id=1, source_target_pairs={{0,4},{4,8},{8,12},{12,16},{16,20},{20,24},{24,28},{1,5},{5,9},{9,... | collective-permute-start | bytes 82952 | tf_op jit(solution)/shard_map/ppermute | solution.py:21
  40.0 1.3 collective-permute-start.6
  41.8 4.1 %collective-permute-done.6 = f32[2,1,3,1152]{3,2,1,0:T(4,128)S(1)} collective-permute-done((f32[2,1,3,1152]{3,2,1,0:T(4,128)S(1)}, f32[2,1,3,1152]{3,2,1,0:T(4,128)S(1)}, u32[]{:S(2)}, u32[]{:S(2)}) %collective-permute-start.6) | collective-permute-done | bytes 27680 | tf_op jit(solution)/shard_map/ppermute | solution.py:24
  48.6 4.3 %collective-permute-start.7 = (f32[2,1,3,1152]{3,2,1,0:T(4,128)S(1)}, f32[2,1,3,1152]{3,2,1,0:T(4,128)S(1)}, u32[]{:S(2)}, u32[]{:S(2)}) collective-permute-start(f32[2,1,3,1152]{3,2,1,0:T(4,128)S(1)} %get-tuple-element.34), channel_id=1, source_target_pairs={{0,4},{4,8},{8,12},{12,16},{16,20},{20,24},{24,28},{1,5},{5,9},{9,... | collective-permute-start | bytes 82952 | tf_op jit(solution)/shard_map/ppermute | solution.py:21
  52.9 1.5 %collective-permute-start.8 = (f32[2,1,3,1152]{3,2,1,0:T(4,128)S(1)}, f32[2,1,3,1152]{3,2,1,0:T(4,128)S(1)}, u32[]{:S(2)}, u32[]{:S(2)}) collective-permute-start(f32[2,1,3,1152]{3,2,1,0:T(4,128)S(1)} %get-tuple-element.35), channel_id=1, source_target_pairs={{4,0},{8,4},{12,8},{16,12},{20,16},{24,20},{28,24},{5,1},{9,5},{13... | collective-permute-start | bytes 82952 | tf_op jit(solution)/shard_map/ppermute | solution.py:24
  54.4 2.0 %copy.56 = f32[2,1,48,1152]{2,0,1,3:T(2,128)S(1)} copy(f32[2,1,48,1152]{3,2,1,0:T(8,128)} %param.7) | data formatting | bytes 884736 | tf_op args[3]
  56.4 2.9 %reshape.594 = f32[4,1,27648]{2,1,0:T(1,128)} reshape(f32[1152,1,2,48]{3,2,1,0:T(2,128)S(1)} %bitcast.40) | data formatting | bytes 884736
  59.3 4.1 %all-to-all-start.1 = ((f32[4,1,27648]{2,1,0:T(1,128)}), f32[4,1,27648]{2,1,0:T(1,128)}, u32[]{:S(2)}, u32[]{:S(2)}) async-start(f32[4,1,27648]{2,1,0:T(1,128)} %reshape.594), calls=%async_computation.1 | async-start | bytes 884736 | tf_op jit(solution)/shard_map/all_to_all | solution.py:130
  65.4 2.8 %reshape.596 = f32[4,1,27648]{2,1,0:T(1,128)} reshape(f32[1152,1,2,48]{3,2,1,0:T(2,128)S(1)} %bitcast.37) | data formatting | bytes 884736
  68.3 3.1 %all-to-all-done.1 = f32[4,1,27648]{2,1,0:T(1,128)} async-done(((f32[4,1,27648]{2,1,0:T(1,128)}), f32[4,1,27648]{2,1,0:T(1,128)}, u32[]{:S(2)}, u32[]{:S(2)}) %all-to-all-start.1) | async-done | bytes 442400 | tf_op jit(solution)/shard_map/all_to_all | solution.py:130
  71.4 4.1 %all-to-all-start = ((f32[4,1,27648]{2,1,0:T(1,128)}), f32[4,1,27648]{2,1,0:T(1,128)}, u32[]{:S(2)}, u32[]{:S(2)}) async-start(f32[4,1,27648]{2,1,0:T(1,128)} %reshape.596), calls=%async_computation | async-start | bytes 884736 | tf_op jit(solution)/shard_map/all_to_all | solution.py:129
  76.0 2.8 %reduce.2 = f32[4,27648]{1,0:T(4,128)S(1)} reduce(f32[4,1,27648]{2,1,0:T(1,128)} %all-to-all-done.1, f32[]{:T(128)} %broadcast.305), dimensions={1}, to_apply=%all_to_all.38.reduce_sub_computation | reduce | bytes 884740 | tf_op jit(solution)/shard_map/all_to_all | solution.py:130
  78.8 1.9 %reshape.595 = f32[1152,1,2,48]{3,2,1,0:T(2,128)S(1)} reshape(f32[4,27648]{1,0:T(4,128)S(1)} %reduce.2) | data formatting | bytes 884736
  81.8 1.7 %all-to-all-done = f32[4,1,27648]{2,1,0:T(1,128)} async-done(((f32[4,1,27648]{2,1,0:T(1,128)}), f32[4,1,27648]{2,1,0:T(1,128)}, u32[]{:S(2)}, u32[]{:S(2)}) %all-to-all-start) | async-done | bytes 442400 | tf_op jit(solution)/shard_map/all_to_all | solution.py:129
  83.5 3.6 %reduce.3 = f32[4,27648]{1,0:T(4,128)} reduce(f32[4,1,27648]{2,1,0:T(1,128)} %all-to-all-done, f32[]{:T(128)} %broadcast.305), dimensions={1}, to_apply=%all_to_all.35.reduce_sub_computation | reduce | bytes 884740 | tf_op jit(solution)/shard_map/all_to_all | solution.py:129
  87.1 2.9 %reshape.597 = f32[1152,1,2,48]{3,2,1,0:T(2,128)S(1)} reshape(f32[4,27648]{1,0:T(4,128)} %reduce.3) | data formatting | bytes 884736
  90.0 1.3 %copy.55 = f32[2,1,48,4,288]{4,2,3,0,1:T(8,128)} copy(f32[2,1,48,4,288]{2,0,4,3,1:T(2,128)S(1)} %bitcast.39) | data formatting | bytes 884736 | tf_op jit(solution)/shard_map/all_to_all | solution.py:129
  91.4 1.5 %reshape.589 = f32[2,4,13824]{2,1,0:T(4,128)S(1)} reshape(f32[2,4,1,48,288]{4,3,1,0,2:T(8,128)} %bitcast.48) | data formatting | bytes 884736 | tf_op jit(solution)/shard_map/reshape | solution.py:105
  96.7 1.3 %add_subtract_fusion = f32[2,4,13824]{2,1,0:T(4,128)} fusion(f32[2,3,13824]{2,1,0:T(4,128)S(1)} %bitcast.52, f32[2,4,13824]{2,1,0:T(4,128)S(1)} %get-tuple-element.7, f32[2,3,13824]{2,1,0:T(4,128)S(1)} %bitcast.46, f32[2,4,13824]{2,1,0:T(4,128)S(1)} %reshape.590), kind=kLoop, calls=%fused_computation.205 | loop fusion | flops 1327104 | bytes 1990656 | tf_op jit(solution)/shard_map/sub | solution.py:96
  98.0 2.3 %reshape.591 = f32[2,4,48,288]{3,2,1,0:T(8,128)} reshape(f32[2,4,13824]{2,1,0:T(4,128)} %add_subtract_fusion) | data formatting | bytes 884736 | tf_op jit(solution)/shard_map/reshape | solution.py:107
  101.4 11.9 %all_to_all.48 = f32[2,4,48,288]{3,2,0,1:T(8,128)S(1)} all-to-all(f32[2,4,48,288]{3,2,0,1:T(8,128)S(1)} %copy.58), channel_id=1, replica_groups=mesh['lat'=8,'lev'=4] {'lev'}, dimensions={1} | all-to-all | bytes 884736 | tf_op jit(solution)/shard_map/all_to_all | solution.py:106
  114.5 1.4 %all_to_all.44 = f32[2,1,48,1152]{3,2,1,0:T(8,128)S(1)} reshape(f32[2,1,48,4,288]{4,3,2,0,1:T(4,128)} %copy.59) | data formatting | bytes 884736 | tf_op jit(solution)/shard_map/all_to_all | solution.py:106
  117.7 4.5 %collective-permute-start.9 = (f32[2,1,3,1152]{3,2,1,0:T(4,128)S(1)}, f32[2,1,3,1152]{3,2,1,0:T(4,128)S(1)}, u32[]{:S(2)}, u32[]{:S(2)}) collective-permute-start(f32[2,1,3,1152]{3,2,1,0:T(4,128)S(1)} %get-tuple-element.30), channel_id=1, source_target_pairs={{0,4},{4,8},{8,12},{12,16},{16,20},{20,24},{24,28},{1,5},{5,9},{9,... | collective-permute-start | bytes 82952 | tf_op jit(solution)/shard_map/ppermute | solution.py:21
  123.5 2.3 %fusion.142 = f32[2,13824]{1,0:T(2,128)S(1)} fusion(f32[2,4,13824]{2,1,0:T(4,128)} %copy-done.4, f32[2,4,13824]{2,1,0:T(4,128)} %copy-done, f32[2,4,13824]{2,1,0:T(4,128)} %copy-done.3, f32[2,4,13824]{2,1,0:T(4,128)S(1)} %get-tuple-element.8, f32[2,4,13824]{2,1,0:T(4,128)} %copy-done.2, f32[2,4,13824]{2,1,0:T(4,128)S(1)} %multiply_multiply_fusion.5), kind=kLoop, calls=%fused_computation.228 | loop fusion | flops 138240 | bytes 774144 | tf_op jit(solution)/shard_map/add | solution.py:97
  126.7 1.4 %collective-permute-done.10 = f32[2,1,3,1152]{3,2,1,0:T(4,128)S(1)} collective-permute-done((f32[2,1,3,1152]{3,2,1,0:T(4,128)S(1)}, f32[2,1,3,1152]{3,2,1,0:T(4,128)S(1)}, u32[]{:S(2)}, u32[]{:S(2)}) %collective-permute-start.10) | collective-permute-done | bytes 27680 | tf_op jit(solution)/shard_map/ppermute | solution.py:24
  (106 shorter events, 30.3 us)
Async XLA Ops:
  0.6 9.1 %copy-start.5 = (f32[1,48,1152]{2,1,0:T(8,128)S(1)}, f32[1,48,1152]{2,1,0:T(8,128)}, u32[]{:S(2)}) copy-start(f32[1,48,1152]{2,1,0:T(8,128)} %param.5) | copy-start | bytes 663556
  0.6 9.0 %copy-start.1 = (f32[2,1,48,1152]{3,2,1,0:T(8,128)S(1)}, f32[2,1,48,1152]{3,2,1,0:T(8,128)}, u32[]{:S(2)}) copy-start(f32[2,1,48,1152]{3,2,1,0:T(8,128)} %param.4) | copy-start | bytes 1327108
  1.8 14.7 %collective-permute-start = (f32[1,1,1152]{2,1,0:T(1,128)S(1)}, f32[1,1,1152]{2,1,0:T(1,128)S(1)}, u32[]{:S(2)}, u32[]{:S(2)}) collective-permute-start(f32[1,1,1152]{2,1,0:T(1,128)S(1)} %slice.702), channel_id=1, source_target_pairs={{0,4},{4,8},{8,12},{12,16},{16,20},{20,24},{24,28},{1,5},{5,9},{9,... | collective-permute-start | bytes 13832 | tf_op jit(solution)/shard_map/ppermute | solution.py:13
  11.4 5.0 %copy-start.6 = (f32[1,48,1152]{2,1,0:T(8,128)S(1)}, f32[1,48,1152]{2,1,0:T(8,128)}, u32[]{:S(2)}) copy-start(f32[1,48,1152]{2,1,0:T(8,128)} %param.6) | copy-start | bytes 663556
  11.7 5.1 %collective-permute-start.1 = (f32[2,1,3,1152]{3,2,1,0:T(4,128)S(1)}, f32[2,1,3,1152]{3,2,1,0:T(4,128)S(1)}, u32[]{:S(2)}, u32[]{:S(2)}) collective-permute-start(f32[2,1,3,1152]{3,2,1,0:T(4,128)S(1)} %get-tuple-element.46), channel_id=1, source_target_pairs={{0,4},{4,8},{8,12},{12,16},{16,20},{20,24},{24,28},{1,5},{5,9},{9,... | collective-permute-start | bytes 82952 | tf_op jit(solution)/shard_map/ppermute | solution.py:21
  15.1 5.9 %collective-permute-start.2 = (f32[2,1,3,1152]{3,2,1,0:T(4,128)S(1)}, f32[2,1,3,1152]{3,2,1,0:T(4,128)S(1)}, u32[]{:S(2)}, u32[]{:S(2)}) collective-permute-start(f32[2,1,3,1152]{3,2,1,0:T(4,128)S(1)} %get-tuple-element.47), channel_id=1, source_target_pairs={{4,0},{8,4},{12,8},{16,12},{20,16},{24,20},{28,24},{5,1},{9,5},{13... | collective-permute-start | bytes 82952 | tf_op jit(solution)/shard_map/ppermute | solution.py:24
  23.7 6.0 %collective-permute-start.3 = (f32[2,1,3,1152]{3,2,1,0:T(4,128)S(1)}, f32[2,1,3,1152]{3,2,1,0:T(4,128)S(1)}, u32[]{:S(2)}, u32[]{:S(2)}) collective-permute-start(f32[2,1,3,1152]{3,2,1,0:T(4,128)S(1)} %get-tuple-element.42), channel_id=1, source_target_pairs={{0,4},{4,8},{8,12},{12,16},{16,20},{20,24},{24,28},{1,5},{5,9},{9,... | collective-permute-start | bytes 82952 | tf_op jit(solution)/shard_map/ppermute | solution.py:21
  28.0 5.9 %collective-permute-start.4 = (f32[2,1,3,1152]{3,2,1,0:T(4,128)S(1)}, f32[2,1,3,1152]{3,2,1,0:T(4,128)S(1)}, u32[]{:S(2)}, u32[]{:S(2)}) collective-permute-start(f32[2,1,3,1152]{3,2,1,0:T(4,128)S(1)} %get-tuple-element.43), channel_id=1, source_target_pairs={{4,0},{8,4},{12,8},{16,12},{20,16},{24,20},{28,24},{5,1},{9,5},{13... | collective-permute-start | bytes 82952 | tf_op jit(solution)/shard_map/ppermute | solution.py:24
  36.6 5.2 %collective-permute-start.5 = (f32[2,1,3,1152]{3,2,1,0:T(4,128)S(1)}, f32[2,1,3,1152]{3,2,1,0:T(4,128)S(1)}, u32[]{:S(2)}, u32[]{:S(2)}) collective-permute-start(f32[2,1,3,1152]{3,2,1,0:T(4,128)S(1)} %get-tuple-element.38), channel_id=1, source_target_pairs={{0,4},{4,8},{8,12},{12,16},{16,20},{20,24},{24,28},{1,5},{5,9},{9,... | collective-permute-start | bytes 82952 | tf_op jit(solution)/shard_map/ppermute | solution.py:21
  40.0 5.9 %collective-permute-start.6 = (f32[2,1,3,1152]{3,2,1,0:T(4,128)S(1)}, f32[2,1,3,1152]{3,2,1,0:T(4,128)S(1)}, u32[]{:S(2)}, u32[]{:S(2)}) collective-permute-start(f32[2,1,3,1152]{3,2,1,0:T(4,128)S(1)} %get-tuple-element.39), channel_id=1, source_target_pairs={{4,0},{8,4},{12,8},{16,12},{20,16},{24,20},{28,24},{5,1},{9,5},{13... | collective-permute-start | bytes 82952 | tf_op jit(solution)/shard_map/ppermute | solution.py:24
  48.6 14.8 %collective-permute-start.7 = (f32[2,1,3,1152]{3,2,1,0:T(4,128)S(1)}, f32[2,1,3,1152]{3,2,1,0:T(4,128)S(1)}, u32[]{:S(2)}, u32[]{:S(2)}) collective-permute-start(f32[2,1,3,1152]{3,2,1,0:T(4,128)S(1)} %get-tuple-element.34), channel_id=1, source_target_pairs={{0,4},{4,8},{8,12},{12,16},{16,20},{20,24},{24,28},{1,5},{5,9},{9,... | collective-permute-start | bytes 82952 | tf_op jit(solution)/shard_map/ppermute | solution.py:21
  52.9 10.5 %collective-permute-start.8 = (f32[2,1,3,1152]{3,2,1,0:T(4,128)S(1)}, f32[2,1,3,1152]{3,2,1,0:T(4,128)S(1)}, u32[]{:S(2)}, u32[]{:S(2)}) collective-permute-start(f32[2,1,3,1152]{3,2,1,0:T(4,128)S(1)} %get-tuple-element.35), channel_id=1, source_target_pairs={{4,0},{8,4},{12,8},{16,12},{20,16},{24,20},{28,24},{5,1},{9,5},{13... | collective-permute-start | bytes 82952 | tf_op jit(solution)/shard_map/ppermute | solution.py:24
  59.3 12.1 %all-to-all-start.1 = ((f32[4,1,27648]{2,1,0:T(1,128)}), f32[4,1,27648]{2,1,0:T(1,128)}, u32[]{:S(2)}, u32[]{:S(2)}) async-start(f32[4,1,27648]{2,1,0:T(1,128)} %reshape.594), calls=%async_computation.1 | async-start | bytes 884736 | tf_op jit(solution)/shard_map/all_to_all | solution.py:130
  71.4 12.1 %all-to-all-start = ((f32[4,1,27648]{2,1,0:T(1,128)}), f32[4,1,27648]{2,1,0:T(1,128)}, u32[]{:S(2)}, u32[]{:S(2)}) async-start(f32[4,1,27648]{2,1,0:T(1,128)} %reshape.596), calls=%async_computation | async-start | bytes 884736 | tf_op jit(solution)/shard_map/all_to_all | solution.py:129
  93.5 0.8 copy-start.2
  94.7 0.8 copy-start.3
  95.5 2.6 %copy-start = (f32[2,4,13824]{2,1,0:T(4,128)}, f32[2,4,13824]{2,1,0:T(4,128)S(1)}, u32[]{:S(2)}) copy-start(f32[2,4,13824]{2,1,0:T(4,128)S(1)} %get-tuple-element.6) | copy-start | bytes 1327108
  95.9 0.8 copy-start.4
  117.7 9.0 %collective-permute-start.9 = (f32[2,1,3,1152]{3,2,1,0:T(4,128)S(1)}, f32[2,1,3,1152]{3,2,1,0:T(4,128)S(1)}, u32[]{:S(2)}, u32[]{:S(2)}) collective-permute-start(f32[2,1,3,1152]{3,2,1,0:T(4,128)S(1)} %get-tuple-element.30), channel_id=1, source_target_pairs={{0,4},{4,8},{8,12},{12,16},{16,20},{20,24},{24,28},{1,5},{5,9},{9,... | collective-permute-start | bytes 82952 | tf_op jit(solution)/shard_map/ppermute | solution.py:21
  122.2 5.9 %collective-permute-start.10 = (f32[2,1,3,1152]{3,2,1,0:T(4,128)S(1)}, f32[2,1,3,1152]{3,2,1,0:T(4,128)S(1)}, u32[]{:S(2)}, u32[]{:S(2)}) collective-permute-start(f32[2,1,3,1152]{3,2,1,0:T(4,128)S(1)} %get-tuple-element.31), channel_id=1, source_target_pairs={{4,0},{8,4},{12,8},{16,12},{20,16},{24,20},{28,24},{5,1},{9,5},{13... | collective-permute-start | bytes 82952 | tf_op jit(solution)/shard_map/ppermute | solution.py:24
where the time goes:
time: 131 us; the launch traced here: 130 us
  starting transfers between devices  39.9 us (30%)
  other arithmetic  28.9 us (22%)
  local copies, waits for them, and re-layouts  28.2 us (22%)
  waiting for transfers between devices  19.6 us (15%)
  blocking collectives  11.9 us (9%)
    ppermute x5, starting transfers between devices, extended(): lax.ppermute(lax.slice_in_dim(block, block.shape[dim] - width, None, axis...  20.1 us
    ppermute x5, waiting for transfers between devices, extended(): lax.ppermute(lax.slice_in_dim(block, 0, width, axis=dim), axis, backward)  14 us
    unnamed x19, local copies, waits for them, and re-layouts  13.3 us
    all_to_all x1, blocking collectives, columns_settle(): lax.all_to_all(settled.reshape(shape_full), 'lev', split_axis=1, concat_a...  11.9 us
    ppermute x5, starting transfers between devices, extended(): lax.ppermute(lax.slice_in_dim(block, 0, width, axis=dim), axis, backward)  6.64 us
    ppermute x1, starting transfers between devices, passed_along(): return lax.ppermute(block, axis, route)  4.9 us
    all_to_all x1, starting transfers between devices, on_device(): lax.all_to_all(fall_speed, 'lev', split_axis=3, concat_axis=1, tiled=True)  4.13 us
    all_to_all x1, starting transfers between devices, on_device(): lax.all_to_all(field, 'lev', split_axis=3, concat_axis=1, tiled=True)  4.12 us
  transfers between devices with their start and end apart: 13, of which 8 were waited for; matrix products, arithmetic and copies ran while one was open for 19% of the time, Pallas kernels for 0%

commit v1 on v0

v1 whole, which is shorter than its diff:
```python
import functools
import jax
import jax.numpy as jnp
from jax import lax
from jax.experimental import pallas as pl
from jax.experimental.pallas import tpu as pltpu
from jax.sharding import PartitionSpec as P

HSUB = 4
SETTLE_SUBSTEPS = 6
SUB = 8
LANE = 128
F32 = jnp.float32


def loop(count, body, unroll=1):
    def step(i, carry):
        body(i)
        return carry

    lax.fori_loop(0, count, step, 0, unroll=unroll)


def group(i):
    if isinstance(i, int):
        return pl.ds(SUB * i, SUB)
    return pl.ds(pl.multiple_of(SUB * i, SUB), SUB)


def roll(x, shift, axis):
    shift %= x.shape[axis]
    return pltpu.roll(x, shift, axis) if shift else x


def sublanes(width):
    return lax.broadcasted_iota(jnp.int32, (SUB, width), 0)


def lanes():
    return lax.broadcasted_iota(jnp.int32, (SUB, LANE), 1)


def coefficients(k):
    s = jnp.abs(k)
    r = 1.0 - s
    ks = k * s
    return k * (r * r), -(ks * r), ks * (3.0 - 2.0 * s)


def face(a, b, c, d):
    interp = (7.0 / 12.0) * (b + c) - (1.0 / 12.0) * (a + d)
    return jnp.minimum(jnp.maximum(interp, jnp.minimum(b, c)), jnp.maximum(b, c))


def swept(q, below2, below, above, co, axis):
    al, be, ga = co
    f = face(below2, below, q, above)
    up = al >= 0
    other = jnp.where(up, roll(f, 1, axis), roll(f, -1, axis))
    w = al * f + be * other + ga * jnp.where(up, below, q)
    return q - (roll(w, -1, axis) - w)


def zonal(q, co):
    return swept(q, roll(q, 2, 1), roll(q, 1, 1), roll(q, -1, 1), co, 1)


class Plan:
    def __init__(self, bins, rows, lons, count):
        self.bins, self.rows, self.lons, self.count = bins, rows, lons, count
        self.groups = rows // SUB
        self.width = lons // count
        self.full, self.rem = divmod(self.width, LANE)
        self.per = LANE // self.rem if self.rem else 1
        cores = bins * self.groups
        rems = (lambda n: -(-n // self.per)) if self.rem else (lambda n: 0)
        self.core_rem = cores * self.full
        self.core = self.core_rem + rems(cores)
        self.halo_rem = self.core + bins * self.full
        self.field = self.halo_rem + rems(bins)
        self.shared = bool(self.rem) and 2 * bins <= self.per
        self.speed_rem = self.field + bins * self.full
        self.total = self.speed_rem + (0 if self.shared else rems(bins))
        self.tiles = lons // LANE
        self.halo_groups = 2 * bins + 3 + (bins + 1) // 2


def window(tiles, start, width, at, cache):
    tile, off = divmod(start, LANE)

    def turned(i):
        key = (i, (at - off) % LANE)
        if key not in cache:
            cache[key] = roll(tiles[i], at - off, 1)
        return cache[key]

    if off + width <= LANE:
        return turned(tile)
    return jnp.where(lanes() < at + LANE - off, turned(tile), turned(tile + 1))


def pack(plan, rows_of, out, tile_at, first_rem):
    held = [None] * plan.count
    for i, tiles in enumerate(rows_of):
        slot = i % plan.per
        cache = {}
        for j in range(plan.count):
            base = j * plan.width
            for t in range(plan.full):
                v = window(tiles, base + LANE * t, LANE, 0, cache)
                out[j, group(tile_at(i) + t), :] = v
            if plan.rem:
                at = plan.rem * slot
                v = window(tiles, base + LANE * plan.full, plan.rem, at, cache)
                held[j] = v if slot == 0 else jnp.where(lanes() < at, held[j], v)
                if slot == plan.per - 1 or i == len(rows_of) - 1:
                    out[j, group(first_rem + i // plan.per), :] = held[j]


def unpack(plan, parts, index, rem_vector, slot):
    tiles = [None] * plan.tiles

    def put(v, start, width, at):
        tile, off = divmod(start, LANE)
        v = roll(v, off - at, 1)
        for t, low, high in ((tile, off, off + width), (tile + 1, 0, off + width - LANE)):
            if high > low:
                tiles[t] = v if low == 0 else jnp.where(lanes() < low, tiles[t], v)

    for j in range(plan.count):
        base = j * plan.width
        for t in range(plan.full):
            put(parts[j, group(index + t), :], base + LANE * t, LANE, 0)
        if plan.rem:
            put(parts[j, group(rem_vector), :], base + LANE * plan.full, plan.rem, plan.rem * slot)
    return tiles


def split(x):
    return [x[:, LANE * t : LANE * (t + 1)] for t in range(x.shape[1] // LANE)]


def start_kernel(plan, tracer, east, north, speed, q1, up, down):
    top, bins = plan.groups - 1, plan.bins
    sub = sublanes(plan.lons)

    def body(g):
        co = coefficients(roll(east[group(g), :], 1, 1))
        for b in range(bins):
            q1[b, group(g), :] = zonal(tracer[b, group(g), :], co)

    loop(plan.groups, body)
    for b in range(bins):
        for half in range(2):
            v = q1[b, group(top - 1 + half), :]
            if b == 0 and half == 0:
                v = jnp.where(sub == 0, roll(north[group(top - 1), :], -3, 0), v)
            up[group(2 * b + half), :] = v
            down[group(2 * b + half), :] = q1[b, group(half), :]
    base = 2 * bins
    up[group(base), :] = east[group(top), :]
    up[group(base + 1), :] = north[group(top), :]
    up[group(base + 2), :] = jnp.where(
        sub < 4, roll(east[group(top - 1), :], 4, 0), north[group(top - 1), :]
    )
    down[group(base), :] = east[group(0), :]
    down[group(base + 1), :] = north[group(0), :]
    down[group(base + 2), :] = jnp.where(sub < 4, east[group(1), :], roll(north[group(1), :], 4, 0))
    for p in range((bins + 1) // 2):
        other = min(2 * p + 1, bins - 1)
        up[group(base + 3 + p), :] = jnp.where(
            sub < 4, roll(speed[other, group(top), :], 4, 0), speed[2 * p, group(top), :]
        )
        down[group(base + 3 + p), :] = jnp.where(
            sub < 4, speed[2 * p, group(0), :], roll(speed[other, group(0), :], 4, 0)
        )


def speed_kernel(plan, speed, *refs):
    outs, chunks = refs[:-1], refs[-1]
    me = lax.axis_index("lev")
    rows_of = [
        split(speed[b, group(g), :]) for b in range(plan.bins) for g in range(plan.groups)
    ]
    pack(plan, rows_of, chunks, lambda i: i * plan.full, plan.core_rem)
    for k in range(plan.count):
        outs[k][...] = chunks[me ^ k]


def advect_kernel(plan, q1, south, above, east, north, *refs):
    outs = refs[: plan.count]
    ce, cn, fa, fb, nraw, chunks = refs[plan.count :]
    bins, groups, tiles = plan.bins, plan.groups, plan.tiles
    frame = groups + 4
    base = 2 * bins
    sub = sublanes(plan.lons)
    me = lax.axis_index("lev")
    last = lax.axis_index("lat") == lax.axis_size("lat") - 1

    for b in range(bins):
        for t in range(tiles):
            cut = slice(LANE * t, LANE * (t + 1))
            for buf in (fa, fb):
                buf[b, t, group(0), :] = jnp.zeros((SUB, LANE), F32)
                buf[b, t, group(frame + 1), :] = jnp.zeros((SUB, LANE), F32)
            for half in range(2):
                fa[b, t, group(1 + half), :] = south[group(2 * b + half), cut]
                fa[b, t, group(3 + groups + half), :] = above[group(2 * b + half), cut]
            fa[b, t, pl.ds(3 * SUB, plan.rows), :] = q1[b, :, cut]

    def put_east(g, value):
        for i, c in enumerate(coefficients(roll(value, 1, 1))):
            ce[i, group(g), :] = c

    put_east(0, roll(south[group(base + 2), :], 4, 0))
    put_east(1, south[group(base), :])
    loop(groups, lambda g: put_east(g + 2, east[group(g), :]))
    put_east(groups + 2, above[group(base), :])
    put_east(groups + 3, above[group(base + 2), :])

    nraw[group(0), :] = jnp.where(
        sub == 3, roll(south[group(0), :], 3, 0), south[group(base + 2), :]
    )
    nraw[group(1), :] = south[group(base + 1), :]
    nraw[pl.ds(2 * SUB, plan.rows - SUB), :] = north[pl.ds(0, plan.rows - SUB), :]
    closed = jnp.logical_and(last, sub == SUB - 1)
    nraw[group(groups + 1), :] = jnp.where(closed, 0.0, north[group(groups - 1), :])
    nraw[group(groups + 2), :] = above[group(base + 1), :]
    nraw[group(groups + 3), :] = roll(above[group(base + 2), :], 4, 0)

    def column(t):
        cut = pl.ds(pl.multiple_of(LANE * t, LANE), LANE)
        for i, c in enumerate(coefficients(roll(nraw[:, cut], 1, 0))):
            cn[i, :, cut] = c

    loop(tiles, column)

    rows = frame * SUB

    def meridional(src, dst):
        def body(t):
            cut = pl.ds(pl.multiple_of(LANE * t, LANE), LANE)
            co = [cn[i, :, cut] for i in range(3)]
            for b in range(bins):
                q, below2, below, beyond = (
                    src[b, t, pl.ds(SUB + d, rows), :] for d in (0, -2, -1, 1)
                )
                dst[b, t, pl.ds(SUB, rows), :] = swept(q, below2, below, beyond, co, 0)

        loop(tiles, body)

    def zonal_rows(src, dst, low, count):
        def body(i):
            g = i + low
            co = [ce[n, group(g), :] for n in range(3)]
            for b in range(bins):
                q = jnp.concatenate([src[b, t, group(g + 1), :] for t in range(tiles)], 1)
                q = zonal(q, co)
                for t in range(tiles):
                    dst[b, t, group(g + 1), :] = q[:, LANE * t : LANE * (t + 1)]

        loop(count, body)

    meridional(fa, fb)
    for step in range(1, HSUB):
        low = 1 if 3 * (step + 1) - 3 >= 8 else 0
        zonal_rows(fb, fa, low, frame - 2 * low)
        meridional(fa, fb)

    cores = [
        [fb[b, t, group(3 + g), :] for t in range(tiles)]
        for b in range(bins)
        for g in range(groups)
    ]
    pack(plan, cores, chunks, lambda i: i * plan.full, plan.core_rem)
    sub1 = sublanes(LANE)
    halos = [
        [
            jnp.where(sub1 < 4, fb[b, t, group(3 + groups), :], fb[b, t, group(2), :])
            for t in range(tiles)
        ]
        for b in range(bins)
    ]
    speeds = []
    for b in range(bins):
        at = base + 3 + b // 2
        v = jnp.where(sub < 4, above[group(at), :], south[group(at), :])
        if b % 2:
            v = jnp.where(sub < 4, roll(above[group(at), :], 4, 0), roll(south[group(at), :], 4, 0))
        speeds.append(split(v))
    halo_at = lambda i: plan.core + i * plan.full
    speed_at = lambda i: plan.field + i * plan.full
    if plan.shared:
        either = lambda i: halo_at(i) if i < bins else speed_at(i - bins)
        pack(plan, halos + speeds, chunks, either, plan.halo_rem)
    else:
        pack(plan, halos, chunks, halo_at, plan.halo_rem)
        pack(plan, speeds, chunks, speed_at, plan.speed_rem)
    for k in range(plan.count):
        outs[k][...] = chunks[me ^ k]


def settle_kernel(plan, *refs):
    n, bins = plan.count, plan.bins
    fields, speeds, deposit = refs[:n], refs[n : 2 * n], refs[2 * n]
    outs = refs[2 * n + 1 : 3 * n + 1]
    fld, fal, res, dep = refs[3 * n + 1 :]
    me = lax.axis_index("lev")
    for k in range(n):
        fld[me ^ k] = fields[k][...]
        fal[me ^ k, pl.ds(0, SUB * plan.core), :] = speeds[k][...]
    tiles = bins * plan.full
    for l in range(n):
        if tiles:
            fal[l, pl.ds(SUB * plan.core, SUB * tiles), :] = fld[
                l, pl.ds(SUB * plan.field, SUB * tiles), :
            ]
        for m in range(plan.field - plan.halo_rem):
            if plan.shared:
                v = roll(fld[l, group(plan.halo_rem), :], -bins * plan.rem, 1)
            else:
                v = fld[l, group(plan.speed_rem + m), :]
            fal[l, group(plan.halo_rem + m), :] = v

    size = next(c for c in (4, 2, 1) if plan.field % c == 0 and c * n <= 16)

    def body(i):
        rows = pl.ds(pl.multiple_of(i * SUB * size, SUB), SUB * size)
        q = [fld[l, rows, :] for l in range(n)]
        v = [fal[l, rows, :] for l in range(n)]
        total = None
        for _ in range(SETTLE_SUBSTEPS):
            inflow = None
            for l in range(n):
                flux = v[l] * (1.0 + 0.5 * jnp.tanh(q[l])) * q[l]
                q[l] = (q[l] if inflow is None else q[l] + inflow) - flux
                inflow = flux
            total = inflow if total is None else total + inflow
        for l in range(n):
            res[l, rows, :] = q[l]
        dep[rows, :] = total

    loop(plan.field // size, body)
    for k in range(n):
        outs[k][...] = res[me ^ k]
    for b in range(bins):
        for g in range(plan.groups):
            i = b * plan.groups + g
            for t in range(plan.full):
                deposit[b, group(g), LANE * t : LANE * (t + 1)] = dep[group(i * plan.full + t), :]
            if plan.rem:
                v = dep[group(plan.core_rem + i // plan.per), :]
                v = roll(v, -plan.rem * (i % plan.per), 1)
                deposit[b, group(g), LANE * plan.full :] = v[:, : plan.rem]


def close_kernel(plan, ce, cn, *refs):
    n, bins, groups, tiles = plan.count, plan.bins, plan.groups, plan.tiles
    ins, out = refs[:n], refs[n]
    parts, frame = refs[n + 1 :]
    me = lax.axis_index("lev")
    for k in range(n):
        parts[me ^ k] = ins[k][...]
    sub = sublanes(plan.lons)

    def swept_rows(b, at, index, rem_vector, slot, co):
        q = jnp.concatenate(unpack(plan, parts, index, rem_vector, slot), 1)
        for t, v in enumerate(split(zonal(q, co))):
            for a in at:
                frame[b, t, group(a), :] = v

    for g in range(groups):
        co = [ce[i, group(g + 2), :] for i in range(3)]
        for b in range(bins):
            i = b * groups + g
            swept_rows(
                b, (g + 2,), i * plan.full, plan.core_rem + i // plan.per, i % plan.per, co
            )
    co = [jnp.where(sub < 4, ce[i, group(groups + 2), :], ce[i, group(1), :]) for i in range(3)]
    for b in range(bins):
        swept_rows(
            b, (1, groups + 2), plan.core + b * plan.full,
            plan.halo_rem + b // plan.per, b % plan.per, co,
        )
    rows = (groups + 2) * SUB

    def body(t):
        cut = pl.ds(pl.multiple_of(LANE * t, LANE), LANE)
        co = [cn[i, pl.ds(SUB, rows), cut] for i in range(3)]
        for b in range(bins):
            q, below2, below, beyond = (
                frame[b, t, pl.ds(SUB + d, rows), :] for d in (0, -2, -1, 1)
            )
            out[b, :, cut] = swept(q, below2, below, beyond, co, 0)[SUB : SUB + plan.rows]

    loop(tiles, body)


def shape(*dims):
    return jax.ShapeDtypeStruct(dims, F32)


def call(kernel, plan, outs, scratch, name):
    return pl.pallas_call(
        functools.partial(kernel, plan), out_shape=outs, scratch_shapes=scratch, name=name
    )


def on_device(tracer, east, north, speed):
    bins, one, rows, lons = tracer.shape
    n, bands = lax.axis_size("lev"), lax.axis_size("lat")
    plan = Plan(bins, rows, lons, n)
    tracer, speed = tracer.reshape(bins, rows, lons), speed.reshape(bins, rows, lons)
    east, north = east.reshape(rows, lons), north.reshape(rows, lons)
    msg = SUB * plan.halo_groups
    frame = SUB * (plan.groups + 4)

    q1, up, down = call(
        start_kernel, plan, (shape(bins, rows, lons), shape(msg, lons), shape(msg, lons)), (),
        "start",
    )(tracer, east, north, speed)
    south = lax.ppermute(up, "lat", [(i, i + 1) for i in range(bands - 1)])
    above = lax.ppermute(down, "lat", [(i + 1, i) for i in range(bands - 1)])

    def exchanged(parts):
        return [parts[0]] + [
            lax.ppermute(parts[k], "lev", [(i, i ^ k) for i in range(n)]) for k in range(1, n)
        ]

    part = shape(SUB * plan.core, LANE)
    speeds = exchanged(
        call(
            speed_kernel, plan, (part,) * n, (pltpu.VMEM((n, SUB * plan.core, LANE), F32),), "speed"
        )(speed)
    )

    part = shape(SUB * plan.total, LANE)
    coef = shape(3, frame, lons)
    buf = pltpu.VMEM((bins, plan.tiles, frame + 2 * SUB, LANE), F32)
    *parts, ce, cn = call(
        advect_kernel, plan, (part,) * n + (coef, coef),
        (buf, buf, pltpu.VMEM((frame, lons), F32), pltpu.VMEM((n, SUB * plan.total, LANE), F32)),
        "advect",
    )(q1, south, above, east, north)
    fields = exchanged(parts)

    part = shape(SUB * plan.field, LANE)
    settled = pltpu.VMEM((n, SUB * plan.field, LANE), F32)
    deposit, *parts = call(
        settle_kernel, plan, (shape(bins, rows, plan.width),) + (part,) * n,
        (
            pltpu.VMEM((n, SUB * plan.total, LANE), F32), settled, settled,
            pltpu.VMEM((SUB * plan.field, LANE), F32),
        ),
        "settle",
    )(*fields, *speeds)
    parts = exchanged(parts)

    out = call(
        close_kernel, plan, shape(bins, rows, lons),
        (settled, pltpu.VMEM((bins, plan.tiles, frame, LANE), F32)), "close",
    )(ce, cn, *parts)
    return out.reshape(bins, one, rows, lons), deposit


def solution(mesh):
    in_specs = (
        P(None, "lev", "lat", None),
        P("lev", "lat", None),
        P("lev", "lat", None),
        P(None, "lev", "lat", None),
    )
    out_specs = (P(None, "lev", "lat", None), P(None, "lat", "lev"))
    return jax.shard_map(
        on_device, mesh=mesh, in_specs=in_specs, out_specs=out_specs, check_vma=False
    )
```

time: 131 us -> 71.7 us (0.55)
  Pallas kernels: 0 us -> 29.8 us
  other arithmetic: 28.9 us -> 0 us
  starting transfers between devices: 39.9 us -> 11.7 us
  local copies, waits for them, and re-layouts: 28.2 us -> 2.21 us
  blocking collectives: 11.9 us -> 0 us
  waiting for transfers between devices: 19.6 us -> 26 us
    pallas_call x0 -> x5, Pallas kernels: none -> 29.8 us  [the longest x1 14.5 us: on_device(): call(advect_kernel, plan, (part,) * n + (coef, coef), (buf, buf, pltpu.VM...]
    ppermute x11, starting transfers between devices: 31.6 us -> 11.7 us  [the longest x9 5.49 us: exchanged(): lax.ppermute(parts[k], 'lev', [(i, i ^ k) for i in range(n)])]
    all_to_all x1 -> x0, blocking collectives: 11.9 us -> none  [columns_settle(): lax.all_to_all(settled.reshape(shape_full), 'lev', split_axis=1, concat_a...]
    ppermute x11, waiting for transfers between devices: 14.8 us -> 26 us  [the longest x9 16.5 us: exchanged(): lax.ppermute(parts[k], 'lev', [(i, i ^ k) for i in range(n)])]
    unnamed x19 -> x26, local copies, waits for them, and re-layouts: 13.3 us -> 2.21 us
    all_to_all x2 -> x0, starting transfers between devices: 8.25 us -> none  [the longest x1 4.13 us: on_device(): lax.all_to_all(fall_speed, 'lev', split_axis=3, concat_axis=1, tiled=True)]
    mul x20 -> x0, other arithmetic: 8.12 us -> none  [the longest x12 4 us: sweep(): face_flux_values = courant * jnp.where(courant >= 0, from_west, from_east)]
    all_to_all x2 -> x0, other arithmetic: 6.39 us -> none  [the longest x1 3.57 us: on_device(): lax.all_to_all(field, 'lev', split_axis=3, concat_axis=1, tiled=True)]
  transfers between devices with their start and end apart: 13 -> 11, of which waited for: 8 -> 5; matrix products, arithmetic and copies ran while one was open for 19% -> 0% of each run, Pallas kernels for 0% -> 23%
where the time goes in v1:
time: 71.7 us; the launch traced here: 70.4 us
  Pallas kernels  29.8 us (42%)
  waiting for transfers between devices  26 us (36%)
  starting transfers between devices  11.7 us (16%)
  local copies, waits for them, and re-layouts  2.21 us (3%)
  between operations  0.72 us (1%)
    ppermute x9, waiting for transfers between devices, exchanged(): lax.ppermute(parts[k], 'lev', [(i, i ^ k) for i in range(n)])  16.5 us
    pallas_call x1, Pallas kernels, on_device(): call(advect_kernel, plan, (part,) * n + (coef, coef), (buf, buf, pltpu.VM...  14.5 us
    ppermute x1, waiting for transfers between devices, on_device(): south = lax.ppermute(up, 'lat', [(i, i + 1) for i in range(bands - 1)])  9.56 us
    pallas_call x1, Pallas kernels, on_device(): call(close_kernel, plan, shape(bins, rows, lons), (settled, pltpu.VMEM((b...  5.93 us
    ppermute x9, starting transfers between devices, exchanged(): lax.ppermute(parts[k], 'lev', [(i, i ^ k) for i in range(n)])  5.49 us
    ppermute x1, starting transfers between devices, on_device(): south = lax.ppermute(up, 'lat', [(i, i + 1) for i in range(bands - 1)])  4.9 us
    pallas_call x1, Pallas kernels, on_device(): call(start_kernel, plan, (shape(bins, rows, lons), shape(msg, lons), shap...  4.05 us
    pallas_call x1, Pallas kernels, on_device(): call(settle_kernel, plan, (shape(bins, rows, plan.width),) + (part,) * n,...  3.3 us
  transfers between devices with their start and end apart: 11, of which 5 were waited for; matrix products, arithmetic and copies ran while one was open for 0% of the time, Pallas kernels for 23%

profile of v1, /device:TPU:0, one launch (start us, length us, event | category | flops | bytes accessed | tf_op | source)
XLA Modules:
  0.0 70.4 jit_solution(8076775015125874055)
XLA Ops:
  0.6 4.1 %start.1 = (f32[2,48,1152]{2,1,0:T(8,128)}, f32[64,1152]{1,0:T(8,128)}, f32[64,1152]{1,0:T(8,128)}) custom-call(f32[2,48,1152]{2,1,0:T(8,128)} %bitcast.14, f32[48,1152]{1,0:T(8,128)} %bitcast.9, f32[48,1152]{1,0:T(8,128)} %bitcast.11, f32[2,48,1152]{2,1,0:T(8,128)} %bitcast.7), custom_call_target="tpu_custom_call" | custom-call | tf_op jit(solution)/shard_map/start/pallas_call | solution.py:418
  4.7 4.9 %collective-permute-start = (f32[64,1152]{1,0:T(8,128)}, f32[64,1152]{1,0:T(8,128)S(1)}, u32[]{:S(2)}, u32[]{:S(2)}) collective-permute-start(f32[64,1152]{1,0:T(8,128)} %get-tuple-element.21), channel_id=1, source_target_pairs={{0,4},{4,8},{8,12},{12,16},{16,20},{20,24},{24,28},{1,5},{5,9},{9,... | collective-permute-start | bytes 884744 | tf_op jit(solution)/shard_map/ppermute | solution.py:422
  9.6 1.3 %collective-permute-start.1 = (f32[64,1152]{1,0:T(8,128)}, f32[64,1152]{1,0:T(8,128)S(1)}, u32[]{:S(2)}, u32[]{:S(2)}) collective-permute-start(f32[64,1152]{1,0:T(8,128)} %get-tuple-element.22), channel_id=1, source_target_pairs={{4,0},{8,4},{12,8},{16,12},{20,16},{24,20},{28,24},{5,1},{9,5},{13... | collective-permute-start | bytes 884744 | tf_op jit(solution)/shard_map/ppermute | solution.py:423
  10.9 2.0 %speed.1 = (f32[216,128]{1,0:T(8,128)}, f32[216,128]{1,0:T(8,128)}, f32[216,128]{1,0:T(8,128)}, f32[216,128]{1,0:T(8,128)}) custom-call(f32[2,48,1152]{2,1,0:T(8,128)} %bitcast.8), custom_call_target="tpu_custom_call" | custom-call | tf_op jit(solution)/shard_map/speed/pallas_call | solution.py:432
  12.9 0.0 collective-permute-start.5
  12.9 9.6 %collective-permute-done.south = f32[64,1152]{1,0:T(8,128)S(1)} collective-permute-done((f32[64,1152]{1,0:T(8,128)}, f32[64,1152]{1,0:T(8,128)S(1)}, u32[]{:S(2)}, u32[]{:S(2)}) %collective-permute-start) | collective-permute-done | bytes 294944 | tf_op jit(solution)/shard_map/ppermute | solution.py:422
  22.5 0.0 collective-permute-done.1.above
  22.5 0.7 %copy-done = f32[64,1152]{1,0:T(8,128)} copy-done((f32[64,1152]{1,0:T(8,128)}, f32[64,1152]{1,0:T(8,128)S(1)}, u32[]{:S(2)}) %copy-start) | copy-done | bytes 294936
  23.2 0.1 copy-done.1
  23.3 14.5 %advect.1 = (f32[288,128]{1,0:T(8,128)}, f32[288,128]{1,0:T(8,128)}, f32[288,128]{1,0:T(8,128)}, f32[288,128]{1,0:T(8,128)}, f32[3,80,1152]{2,1,0:T(8,128)}, /*index=5*/f32[3,80,1152]{2,1,0:T(8,128)}) custom-call(f32[2,48,1152]{2,1,0:T(8,128)} %get-tuple-element.20.q1, f32[64,1152]{1,0:T(8,128)} %copy-done, f32[64,1152]{1,0:T(8,128)} %copy-done.1, ...), custom_call_target="tpu_custom_call" | custom-call | tf_op jit(solution)/shard_map/advect/pallas_call | solution.py:440
  37.8 0.0 collective-permute-start.2
  37.8 1.6 %collective-permute-start.3 = (f32[288,128]{1,0:T(8,128)}, f32[288,128]{1,0:T(8,128)S(1)}, u32[]{:S(2)}, u32[]{:S(2)}) collective-permute-start(f32[288,128]{1,0:T(8,128)} %get-tuple-element.27), channel_id=1, source_target_pairs={{0,2},{1,3},{2,0},{3,1},{4,6},{5,7},{6,4},{7,5},{8,10},{9,11},{10,... | collective-permute-start | bytes 442376 | tf_op jit(solution)/shard_map/ppermute | solution.py:427
  39.3 0.3 collective-permute-start.4
  39.6 1.5 %collective-permute-start.6 = (f32[216,128]{1,0:T(8,128)S(1)}, f32[216,128]{1,0:T(8,128)S(1)}, u32[]{:S(2)}, u32[]{:S(2)}) collective-permute-start(f32[216,128]{1,0:T(8,128)S(1)} %copy-done.12), channel_id=1, source_target_pairs={{0,2},{1,3},{2,0},{3,1},{4,6},{5,7},{6,4},{7,5},{8,10},{9,11},{10,... | collective-permute-start | bytes 331784 | tf_op jit(solution)/shard_map/ppermute | solution.py:427
  41.1 0.0 collective-permute-done.5.refs_5_
  41.1 0.3 collective-permute-start.7
  41.4 8.9 %collective-permute-done.6.refs_6_ = f32[216,128]{1,0:T(8,128)S(1)} collective-permute-done((f32[216,128]{1,0:T(8,128)S(1)}, f32[216,128]{1,0:T(8,128)S(1)}, u32[]{:S(2)}, u32[]{:S(2)}) %collective-permute-start.6) | collective-permute-done | bytes 110624 | tf_op jit(solution)/shard_map/ppermute | solution.py:427
  50.3 1.3 %collective-permute-done.7.refs_7_ = f32[216,128]{1,0:T(8,128)S(1)} collective-permute-done((f32[216,128]{1,0:T(8,128)S(1)}, f32[216,128]{1,0:T(8,128)S(1)}, u32[]{:S(2)}, u32[]{:S(2)}) %collective-permute-start.7) | collective-permute-done | bytes 110624 | tf_op jit(solution)/shard_map/ppermute | solution.py:427
  51.6 0.0 collective-permute-done.3.refs_2_
  51.7 0.6 copy-done.10
  52.3 0.0 copy-done.2
  52.3 0.0 copy-done.3
  52.4 0.0 copy-done.4
  52.4 3.3 %settle.1 = (f32[2,48,288]{2,1,0:T(8,128)}, f32[256,128]{1,0:T(8,128)}, f32[256,128]{1,0:T(8,128)}, f32[256,128]{1,0:T(8,128)}, f32[256,128]{1,0:T(8,128)}) custom-call(f32[288,128]{1,0:T(8,128)} %get-tuple-element.25.refs_0_, f32[288,128]{1,0:T(8,128)} %copy-done.2, f32[288,128]{1,0:T(8,128)} %copy-done.3, f32[288,128]{1,0:T(8,128)} %copy-done.4, ...), custom_call_target="tpu_custom_call" | custom-call | tf_op jit(solution)/shard_map/settle/pallas_call | solution.py:449
  55.7 0.4 collective-permute-start.8
  56.1 1.5 %collective-permute-start.9 = (f32[256,128]{1,0:T(8,128)}, f32[256,128]{1,0:T(8,128)S(1)}, u32[]{:S(2)}, u32[]{:S(2)}) collective-permute-start(f32[256,128]{1,0:T(8,128)} %get-tuple-element.35), channel_id=1, source_target_pairs={{0,2},{1,3},{2,0},{3,1},{4,6},{5,7},{6,4},{7,5},{8,10},{9,11},{10,... | collective-permute-start | bytes 393224 | tf_op jit(solution)/shard_map/ppermute | solution.py:427
  57.6 0.0 collective-permute-start.10
  57.6 0.0 collective-permute-done.8.refs_1_
  57.6 5.1 %collective-permute-done.9.refs_2_ = f32[256,128]{1,0:T(8,128)S(1)} collective-permute-done((f32[256,128]{1,0:T(8,128)}, f32[256,128]{1,0:T(8,128)S(1)}, u32[]{:S(2)}, u32[]{:S(2)}) %collective-permute-start.9) | collective-permute-done | bytes 131104 | tf_op jit(solution)/shard_map/ppermute | solution.py:427
  62.7 1.2 %collective-permute-done.10.refs_3_ = f32[256,128]{1,0:T(8,128)S(1)} collective-permute-done((f32[256,128]{1,0:T(8,128)}, f32[256,128]{1,0:T(8,128)S(1)}, u32[]{:S(2)}, u32[]{:S(2)}) %collective-permute-start.10) | collective-permute-done | bytes 131104 | tf_op jit(solution)/shard_map/ppermute | solution.py:427
  63.8 0.6 copy-done.7
  64.5 5.9 %close.1 = f32[2,48,1152]{2,1,0:T(8,128)} custom-call(f32[3,80,1152]{2,1,0:T(8,128)} %get-tuple-element.23.ce, f32[3,80,1152]{2,1,0:T(8,128)} %get-tuple-element.24.cn, f32[256,128]{1,0:T(8,128)} %get-tuple-element.33.refs_0_, f32[256,128]{1,0:T(8,128)} %copy-done.5, f32[256,128]{1,0:T(8,128)} %copy-done.6, f32[256,128]{1,0:T(8,128)} %copy-done.7), custom_call_target="tpu_custom_call" | custom-call | tf_op jit(solution)/shard_map/close/pallas_call | solution.py:459
  (21 shorter events, 0.0 us)
Async XLA Ops:
  4.7 17.8 %collective-permute-start = (f32[64,1152]{1,0:T(8,128)}, f32[64,1152]{1,0:T(8,128)S(1)}, u32[]{:S(2)}, u32[]{:S(2)}) collective-permute-start(f32[64,1152]{1,0:T(8,128)} %get-tuple-element.21), channel_id=1, source_target_pairs={{0,4},{4,8},{8,12},{12,16},{16,20},{20,24},{24,28},{1,5},{5,9},{9,... | collective-permute-start | bytes 884744 | tf_op jit(solution)/shard_map/ppermute | solution.py:422
  9.6 12.9 %collective-permute-start.1 = (f32[64,1152]{1,0:T(8,128)}, f32[64,1152]{1,0:T(8,128)S(1)}, u32[]{:S(2)}, u32[]{:S(2)}) collective-permute-start(f32[64,1152]{1,0:T(8,128)} %get-tuple-element.22), channel_id=1, source_target_pairs={{4,0},{8,4},{12,8},{16,12},{20,16},{24,20},{28,24},{5,1},{9,5},{13... | collective-permute-start | bytes 884744 | tf_op jit(solution)/shard_map/ppermute | solution.py:423
  12.9 26.8 %copy-start.12 = (f32[216,128]{1,0:T(8,128)S(1)}, f32[216,128]{1,0:T(8,128)}, u32[]{:S(2)}) copy-start(f32[216,128]{1,0:T(8,128)} %get-tuple-element.31) | copy-start | bytes 331780
  12.9 28.3 %copy-start.11 = (f32[216,128]{1,0:T(8,128)S(1)}, f32[216,128]{1,0:T(8,128)}, u32[]{:S(2)}) copy-start(f32[216,128]{1,0:T(8,128)} %get-tuple-element.32) | copy-start | bytes 331780
  12.9 28.3 %collective-permute-start.5 = (f32[216,128]{1,0:T(8,128)}, f32[216,128]{1,0:T(8,128)S(1)}, u32[]{:S(2)}, u32[]{:S(2)}) collective-permute-start(f32[216,128]{1,0:T(8,128)} %get-tuple-element.30), channel_id=1, source_target_pairs={{0,1},{1,0},{2,3},{3,2},{4,5},{5,4},{6,7},{7,6},{8,9},{9,8},{10,11... | collective-permute-start | bytes 331784 | tf_op jit(solution)/shard_map/ppermute | solution.py:427
  22.5 0.7 %copy-start = (f32[64,1152]{1,0:T(8,128)}, f32[64,1152]{1,0:T(8,128)S(1)}, u32[]{:S(2)}) copy-start(f32[64,1152]{1,0:T(8,128)S(1)} %collective-permute-done.south) | copy-start | bytes 884740
  22.5 0.8 %copy-start.1 = (f32[64,1152]{1,0:T(8,128)}, f32[64,1152]{1,0:T(8,128)S(1)}, u32[]{:S(2)}) copy-start(f32[64,1152]{1,0:T(8,128)S(1)} %collective-permute-done.1.above) | copy-start | bytes 884740
  37.8 13.8 %collective-permute-start.2 = (f32[288,128]{1,0:T(8,128)}, f32[288,128]{1,0:T(8,128)S(1)}, u32[]{:S(2)}, u32[]{:S(2)}) collective-permute-start(f32[288,128]{1,0:T(8,128)} %get-tuple-element.26), channel_id=1, source_target_pairs={{0,1},{1,0},{2,3},{3,2},{4,5},{5,4},{6,7},{7,6},{8,9},{9,8},{10,11... | collective-permute-start | bytes 442376 | tf_op jit(solution)/shard_map/ppermute | solution.py:427
  37.8 13.8 %collective-permute-start.3 = (f32[288,128]{1,0:T(8,128)}, f32[288,128]{1,0:T(8,128)S(1)}, u32[]{:S(2)}, u32[]{:S(2)}) collective-permute-start(f32[288,128]{1,0:T(8,128)} %get-tuple-element.27), channel_id=1, source_target_pairs={{0,2},{1,3},{2,0},{3,1},{4,6},{5,7},{6,4},{7,5},{8,10},{9,11},{10,... | collective-permute-start | bytes 442376 | tf_op jit(solution)/shard_map/ppermute | solution.py:427
  39.3 12.3 %collective-permute-start.4 = (f32[288,128]{1,0:T(8,128)}, f32[288,128]{1,0:T(8,128)S(1)}, u32[]{:S(2)}, u32[]{:S(2)}) collective-permute-start(f32[288,128]{1,0:T(8,128)} %get-tuple-element.28), channel_id=1, source_target_pairs={{0,3},{1,2},{2,1},{3,0},{4,7},{5,6},{6,5},{7,4},{8,11},{9,10},{10,... | collective-permute-start | bytes 442376 | tf_op jit(solution)/shard_map/ppermute | solution.py:427
  39.6 10.7 %collective-permute-start.6 = (f32[216,128]{1,0:T(8,128)S(1)}, f32[216,128]{1,0:T(8,128)S(1)}, u32[]{:S(2)}, u32[]{:S(2)}) collective-permute-start(f32[216,128]{1,0:T(8,128)S(1)} %copy-done.12), channel_id=1, source_target_pairs={{0,2},{1,3},{2,0},{3,1},{4,6},{5,7},{6,4},{7,5},{8,10},{9,11},{10,... | collective-permute-start | bytes 331784 | tf_op jit(solution)/shard_map/ppermute | solution.py:427
  41.1 10.5 %copy-start.8 = (f32[216,128]{1,0:T(8,128)}, f32[216,128]{1,0:T(8,128)S(1)}, u32[]{:S(2)}) copy-start(f32[216,128]{1,0:T(8,128)S(1)} %collective-permute-done.5.refs_5_) | copy-start | bytes 331780
  41.1 10.5 %collective-permute-start.7 = (f32[216,128]{1,0:T(8,128)S(1)}, f32[216,128]{1,0:T(8,128)S(1)}, u32[]{:S(2)}, u32[]{:S(2)}) collective-permute-start(f32[216,128]{1,0:T(8,128)S(1)} %copy-done.11), channel_id=1, source_target_pairs={{0,3},{1,2},{2,1},{3,0},{4,7},{5,6},{6,5},{7,4},{8,11},{9,10},{10,... | collective-permute-start | bytes 331784 | tf_op jit(solution)/shard_map/ppermute | solution.py:427
  50.3 1.4 %copy-start.9 = (f32[216,128]{1,0:T(8,128)}, f32[216,128]{1,0:T(8,128)S(1)}, u32[]{:S(2)}) copy-start(f32[216,128]{1,0:T(8,128)S(1)} %collective-permute-done.6.refs_6_) | copy-start | bytes 331780
  51.6 0.7 copy-start.10
  51.6 0.7 copy-start.2
  51.6 0.7 %copy-start.3 = (f32[288,128]{1,0:T(8,128)}, f32[288,128]{1,0:T(8,128)S(1)}, u32[]{:S(2)}) copy-start(f32[288,128]{1,0:T(8,128)S(1)} %collective-permute-done.3.refs_2_) | copy-start | bytes 442372
  51.7 0.8 %copy-start.4 = (f32[288,128]{1,0:T(8,128)}, f32[288,128]{1,0:T(8,128)S(1)}, u32[]{:S(2)}) copy-start(f32[288,128]{1,0:T(8,128)S(1)} %collective-permute-done.4.refs_3_) | copy-start | bytes 442372
  55.7 1.9 %collective-permute-start.8 = (f32[256,128]{1,0:T(8,128)}, f32[256,128]{1,0:T(8,128)S(1)}, u32[]{:S(2)}, u32[]{:S(2)}) collective-permute-start(f32[256,128]{1,0:T(8,128)} %get-tuple-element.34), channel_id=1, source_target_pairs={{0,1},{1,0},{2,3},{3,2},{4,5},{5,4},{6,7},{7,6},{8,9},{9,8},{10,11... | collective-permute-start | bytes 393224 | tf_op jit(solution)/shard_map/ppermute | solution.py:427
  56.1 6.6 %collective-permute-start.9 = (f32[256,128]{1,0:T(8,128)}, f32[256,128]{1,0:T(8,128)S(1)}, u32[]{:S(2)}, u32[]{:S(2)}) collective-permute-start(f32[256,128]{1,0:T(8,128)} %get-tuple-element.35), channel_id=1, source_target_pairs={{0,2},{1,3},{2,0},{3,1},{4,6},{5,7},{6,4},{7,5},{8,10},{9,11},{10,... | collective-permute-start | bytes 393224 | tf_op jit(solution)/shard_map/ppermute | solution.py:427
  57.6 6.3 %collective-permute-start.10 = (f32[256,128]{1,0:T(8,128)}, f32[256,128]{1,0:T(8,128)S(1)}, u32[]{:S(2)}, u32[]{:S(2)}) collective-permute-start(f32[256,128]{1,0:T(8,128)} %get-tuple-element.36), channel_id=1, source_target_pairs={{0,3},{1,2},{2,1},{3,0},{4,7},{5,6},{6,5},{7,4},{8,11},{9,10},{10,... | collective-permute-start | bytes 393224 | tf_op jit(solution)/shard_map/ppermute | solution.py:427
  57.6 6.3 %copy-start.5 = (f32[256,128]{1,0:T(8,128)}, f32[256,128]{1,0:T(8,128)S(1)}, u32[]{:S(2)}) copy-start(f32[256,128]{1,0:T(8,128)S(1)} %collective-permute-done.8.refs_1_) | copy-start | bytes 393220
  62.7 1.2 %copy-start.6 = (f32[256,128]{1,0:T(8,128)}, f32[256,128]{1,0:T(8,128)S(1)}, u32[]{:S(2)}) copy-start(f32[256,128]{1,0:T(8,128)S(1)} %collective-permute-done.9.refs_2_) | copy-start | bytes 393220
  63.8 0.6 copy-start.7
